TPU v7x, 32 devices: a whole 2x2x4 slice. The times are simulated.
32 devices in a mesh: groups: 2 (over y), wide: 4 (over x, core), narrow: 4 (over z).
Axes of the slice: x: 2, y: 2, z: 4, core: 2. Of those that a mesh axis runs over, the one named last changes fastest.
Arguments:
- spectra: bfloat16 [2, 32, 640, 2, 1281], P(None, ('groups', 'wide'), 'narrow'), parts along dimension 1, may hold values from -6 to 6
- legendre: bfloat16 [320, 1281, 128], P('narrow'), may hold values from -0.15625 to 0.15625
- pair_of_slot: int32 [640], replicated, may hold values from 0 to 639, each once
- lat_owner: int32 [128], replicated, may hold values from 0 to 3, as said below
- region_of_lon: int32 [2048], replicated, may hold values from 0 to 63, never falling along the last dimension, each value on 1 to 48 neighbouring positions
Outputs:
- peak: float32 [4, 128, 64], P('groups', 'narrow', 'wide'), parts along dimension 0
- peak_slope: float32 [4, 128, 64], P('groups', 'narrow', 'wide'), parts along dimension 0
There are 2 independent parts, one for each index of `groups`. A program takes and returns all parts, laid end to end along the dimension named above; an argument that names none is the same for every part. Nothing has to cross between parts.
Inputs may be any that keep to these rules, and one draw needn't show every extreme that they name: `lat_owner`: each index of narrow owns exactly 32 latitudes. `region_of_lon`: regions never fall along the longitudes and every region has at least one longitude. `pair_of_slot`: a permutation.
All inputs are finite; a program needn't handle non-finite values.
Results may differ from a plain program's by a relative error of at most 0.0003.
Values sent between devices are 32-bit elements; how exact they have to be, the bound alone decides.
A program may use at most 192 MiB of HBM per device.

v0:
```python
import functools
import math

import jax
import jax.numpy as jnp
from jax import lax
from jax.experimental import pallas as pl
from jax.experimental.pallas import tpu as pltpu
from jax.sharding import PartitionSpec as P

M = 1280
LON = 2048
REG_DEV = 16
LON_FULL = 5120


def synthesize(operand, waves, start, width):
    columns = start + jnp.arange(width, dtype=jnp.int32)
    phase = waves[:, None] * columns[None, :] % LON_FULL
    angle = phase.astype(jnp.float32) * (2.0 * math.pi / LON_FULL)
    cosine = jnp.cos(angle)
    sine = jnp.sin(angle)
    rate = (waves.astype(jnp.float32) / M)[:, None]
    upper = jnp.concatenate([cosine, -rate * sine], axis=1)
    lower = jnp.concatenate([-sine, -rate * cosine], axis=1)
    table = jnp.concatenate([upper, lower], axis=0) * M ** (-0.5)
    return jnp.dot(operand, table, precision=lax.Precision.HIGHEST)


def synthesize_all(operand, waves):
    width = min(512, LON)
    starts = jnp.arange(LON // width, dtype=jnp.int32) * width

    def one_block(begin):
        return synthesize(operand, waves, begin, width)

    blocks = lax.map(one_block, starts)
    blocks = blocks.reshape(blocks.shape[0], blocks.shape[1], 2, width)
    value = jnp.transpose(blocks[:, :, 0], (1, 0, 2)).reshape(operand.shape[0], LON)
    slope = jnp.transpose(blocks[:, :, 1], (1, 0, 2)).reshape(operand.shape[0], LON)
    return (value, slope)


def region_peak(values, region_of_lon, wanted):
    hits = region_of_lon[:, None] == wanted[None, :]
    masked = jnp.where(hits[None, None], values[..., None], -1e30)
    return masked.max(axis=2)


def per_device_plain(spectra, legendre, pair_of_slot, lat_owner, region_of_lon):
    members = spectra.shape[0]
    steps_here = spectra.shape[1]
    slot_count = spectra.shape[2]
    length = spectra.shape[4]
    half_count = legendre.shape[0]
    lat_half = legendre.shape[2] // 2
    here = lax.axis_index("narrow")
    paired = lax.dynamic_slice_in_dim(pair_of_slot, here * slot_count, slot_count)
    position = jnp.arange(length, dtype=jnp.int32)[None, :]
    first_len = (M - paired)[:, None]
    leading = position < first_len
    offset = jnp.where(leading, position, position - first_len)
    even_term = offset % 2 == 0
    masks = jnp.stack(
        [leading & even_term, leading & ~even_term, ~leading & even_term, ~leading & ~even_term],
        axis=1,
    ).astype(jnp.bfloat16)
    ordered = jnp.transpose(spectra, (2, 0, 1, 3, 4))
    masked = masks[:, :, None, None, None, :] * ordered[:, None]
    masked = masked.reshape(half_count, 2, -1, length)
    table = legendre.reshape(half_count, length, 2, lat_half)
    sums = jnp.einsum("abrl,albj->abrj", masked, table, preferred_element_type=jnp.float32)
    sums = sums.reshape(slot_count, 4, members, steps_here, 2, lat_half)
    north_lead = sums[:, 0] + sums[:, 1]
    south_lead = sums[:, 0] - sums[:, 1]
    north_tail = sums[:, 2] + sums[:, 3]
    south_tail = sums[:, 2] - sums[:, 3]
    lead = jnp.concatenate([north_lead, jnp.flip(south_lead, axis=-1)], axis=-1)
    tail = jnp.concatenate([north_tail, jnp.flip(south_tail, axis=-1)], axis=-1)
    waved = jnp.stack([lead, tail], axis=1).reshape(2 * slot_count, members, steps_here, 2, -1)
    order = jnp.argsort(lat_owner, stable=True)
    waved = jnp.take(waved, order, axis=4)
    arrived = lax.all_to_all(waved, "narrow", split_axis=4, concat_axis=0, tiled=True)
    waves = jnp.stack([pair_of_slot, M - 1 - pair_of_slot], axis=1).reshape(-1)
    lat_here = arrived.shape[4]
    operand = jnp.transpose(arrived, (1, 2, 4, 3, 0)).reshape(members * steps_here * lat_here, -1)
    value, slope = synthesize_all(operand, waves)
    value = value.reshape(members, steps_here, lat_here, LON).max(axis=1)
    slope = jnp.abs(slope).reshape(members, steps_here, lat_here, LON).max(axis=1)
    wide_count = lax.axis_size("wide")
    mine_start = lax.axis_index("wide") * REG_DEV
    wanted = jnp.arange(REG_DEV * wide_count, dtype=jnp.int32)
    peaks = region_peak(value, region_of_lon, wanted)
    slopes = region_peak(slope, region_of_lon, wanted)
    peaks, slopes = lax.pmax((peaks, slopes), "wide")
    peak = lax.dynamic_slice_in_dim(peaks, mine_start, REG_DEV, 2)
    peak_slope = lax.dynamic_slice_in_dim(slopes, mine_start, REG_DEV, 2)
    return (peak, peak_slope)


CHUNK = 16
HALF = 8
FINE = 32
GROUP = 256
MESH = pl.DeviceIdType.MESH


def split(values):
    high = values.astype(jnp.bfloat16)
    low = (values - high.astype(jnp.float32)).astype(jnp.bfloat16)
    return high, low


def dot(left, right):
    return jnp.dot(left, right, preferred_element_type=jnp.float32)


def turn(count):
    quarter = LON_FULL // 2
    whole = jnp.floor(count * (1.0 / quarter) + 0.5)
    angle = (count - whole * quarter) * (math.pi / LON_FULL)
    square = angle * angle
    sine = angle * (1.0 + square * (-1 / 6 + square * (1 / 120 + square * (-1 / 5040 + square * (1 / 362880)))))
    cosine = 1.0 + square * (
        -1 / 2 + square * (1 / 24 + square * (-1 / 720 + square * (1 / 40320 + square * (-1 / 3628800))))
    )
    turns = whole.astype(jnp.int32)
    swap = (turns & 1) == 1
    cos_sign = jnp.where(((turns + 1) & 2) == 2, -1.0, 1.0)
    sin_sign = jnp.where((turns & 2) == 2, -1.0, 1.0)
    return cos_sign * jnp.where(swap, sine, cosine), sin_sign * jnp.where(swap, cosine, sine)


def iota(shape, dim):
    return lax.broadcasted_iota(jnp.int32, shape, dim)


def fields_kernel(
    dims, pair_ref, owner_ref, region_ref, x_hbm, table_hbm, out_ref,
    table_buf, x_buf, lined, spread, sums, place, sent, held, coef, coarse, fine, part_cos, part_sin, field,
    apart, apart_blocks, pick, pick_blocks, absent, peaks, peaks_in,
    fetch_sem, send_sem, recv_sem, wide_send, wide_recv,
):
    narrow, wide, chunks, rows, members, steps_here, lat_here, lon = dims
    me = lax.axis_index("narrow")
    me_wide = lax.axis_index("wide")
    slot_count = chunks * CHUNK
    pairs = CHUNK // 2
    half_lon = lon // 2
    lat = narrow * lat_here

    def fetches(c, slot):
        return (
            pltpu.make_async_copy(
                table_hbm.at[:, pl.ds(pl.multiple_of(c * pairs, pairs), pairs), :], table_buf.at[slot],
                fetch_sem.at[0, slot],
            ),
            pltpu.make_async_copy(
                x_hbm.at[:, :, pl.ds(c * CHUNK, CHUNK), :, :], x_buf.at[slot], fetch_sem.at[1, slot]
            ),
        )

    def start_fetch(c, slot):
        for copy in fetches(c, slot):
            copy.start()

    def partner(ahead):
        return lax.rem(me + ahead, narrow)

    order = (2, 1, 3) if narrow == 4 else tuple(range(1, narrow))

    def send(c, ahead, h):
        target = partner(ahead)
        span = pl.ds(0, 2 * CHUNK) if h is None else pl.ds(h * CHUNK, CHUNK)
        at = 0 if h is None else h
        return pltpu.make_async_remote_copy(
            src_ref=sent.at[c, target, span], dst_ref=held.at[c, me, span],
            send_sem=send_sem.at[at, c, target], recv_sem=recv_sem.at[at, c, me],
            device_id={"narrow": target}, device_id_type=MESH,
        )

    def receive(c, ahead, h):
        origin = partner(ahead)
        span = pl.ds(0, 2 * CHUNK) if h is None else pl.ds(h * CHUNK, CHUNK)
        at = 0 if h is None else h
        return pltpu.make_async_remote_copy(
            src_ref=sent.at[c, origin, span], dst_ref=held.at[c, origin, span],
            send_sem=send_sem.at[at, c, origin], recv_sem=recv_sem.at[at, c, origin],
            device_id={"narrow": origin}, device_id_type=MESH,
        )

    start_fetch(0, 0)
    barrier = pltpu.get_barrier_semaphore()
    for ahead in range(1, narrow):
        pl.semaphore_signal(barrier, inc=1, device_id={"narrow": partner(ahead)}, device_id_type=MESH)
    for ahead in range(1, wide):
        pl.semaphore_signal(
            barrier, inc=1, device_id={"wide": lax.rem(me_wide + ahead, wide)}, device_id_type=MESH
        )

    lane = iota((lat, lat), 1)
    below = iota((lat, lat), 0)
    below = jnp.where(below < lat // 2, below, 3 * lat // 2 - 1 - below)
    owners = jnp.broadcast_to(owner_ref[...], (lat, lat)).astype(jnp.float32)
    owner = jnp.sum(jnp.where(lane == below, owners, 0.0), axis=1, keepdims=True)
    ahead_of = (owners < owner) | ((owners == owner) & (lane < below))
    rank = jnp.sum(jnp.where(ahead_of, 1.0, 0.0), axis=1, keepdims=True).astype(jnp.int32)
    column = iota((lat, narrow * 128), 1)
    goal = (column // 128) * lat_here + column % lat_here
    for n in range(2 * members):
        wanted = (goal == rank) & ((column // lat_here) % (2 * members) == n)
        place[n * lat:(n + 1) * lat, :] = jnp.where(wanted, 1.0, 0.0).astype(jnp.bfloat16)

    position = iota((1, M), 1)
    half_lane = iota((rows, 128), 1)
    block = M // 8

    def one_pair(c, slot, at, u):
        parts = []
        extras = []
        for half in range(2):
            inside = 2 * at + half
            lines = 2 * u + half
            first_len = M - pair_ref[me * slot_count + c * CHUNK + inside]
            leading = (position < first_len).astype(jnp.float32)
            trailing = 1.0 - leading
            sign_lead = (1 - 2 * (position & 1)).astype(jnp.float32)
            flip = (1 - 2 * (first_len & 1)).astype(jnp.float32)
            for e in range(members):
                for t in range(steps_here):
                    row = 2 * (e * steps_here + t)
                    lined[lines, row:row + 2, :] = x_buf[slot, e, t, inside].astype(jnp.float32)
            body = lined[lines, :, :M].astype(jnp.bfloat16)
            for mask in (leading, leading * sign_lead, trailing, trailing * (sign_lead * flip)):
                parts.append(body * mask.astype(jnp.bfloat16))
            last = lined[lines, :, M:]
            extras.append((last, flip))
        table = spread[pl.ds(at, M, stride=pairs), :].astype(jnp.bfloat16)
        out = dot(jnp.concatenate(parts, axis=0), table)
        edge = spread[pl.ds(M * pairs + at, 1), :]
        for half in range(2):
            base = half * 4 * rows
            piece = [out[base + v * rows:base + (v + 1) * rows] for v in range(4)]
            last, flip = extras[half]
            term = last * edge
            piece[2] = piece[2] + term
            piece[3] = piece[3] + term * flip
            for tail_at in range(2):
                north, south = piece[2 * tail_at], piece[2 * tail_at + 1]
                if half == 0:
                    both = jnp.where(half_lane < 64, north, pltpu.roll(south, 64, 1))
                else:
                    both = jnp.where(half_lane < 64, pltpu.roll(north, 64, 1), south)
                at_row = (tail_at * HALF + 2 * u + half) * rows
                sums[at_row:at_row + rows, :] = both

    def one_half(c, slot, h):
        for u in range(HALF // 2):
            one_pair(c, slot, h * (HALF // 2) + u, u)
        highs, lows = [], []
        for t in range(steps_here):
            wide_rows = jnp.concatenate(
                [
                    sums[pl.ds((e * steps_here + t) * 2 + part, CHUNK, stride=rows), :]
                    for part in range(2) for e in range(members)
                ],
                axis=1,
            )
            high, low = split(wide_rows)
            highs.append(high)
            lows.append(low)
        both = dot(jnp.concatenate(highs + lows, axis=0), place[...])
        moved = both[:steps_here * CHUNK] + both[steps_here * CHUNK:]
        where_to = pl.ds(pl.multiple_of(h * CHUNK, CHUNK), CHUNK)
        for t in range(steps_here):
            for d in range(narrow):
                sent[c, d, where_to, t * 128:(t + 1) * 128] = (
                    moved[t * CHUNK:(t + 1) * CHUNK, d * 128:(d + 1) * 128]
                )
        held[c, me, where_to, :] = sent[c, me, where_to, :]

        @pl.when((c == 0) & (h == 0))
        def _():
            pl.semaphore_wait(barrier, narrow - 1 + wide - 1)
            for ahead in order:
                send(0, ahead, 0).start()

        @pl.when((c == 0) & (h == 1))
        def _():
            for ahead in order:
                send(0, ahead, 1).start()

        @pl.when((c == chunks - 1) & (h == 0))
        def _():
            for ahead in order:
                send(chunks - 1, ahead, 0).start()

        @pl.when((c == chunks - 1) & (h == 1))
        def _():
            for ahead in order:
                send(chunks - 1, ahead, 1).start()

        @pl.when((c > 0) & (c < chunks - 1) & (h == 1))
        def _():
            for ahead in order:
                send(c, ahead, None).start()

    def tables(c):
        lanes = iota((8, 128), 1)
        base = lanes & ~HALF
        lead = jnp.zeros((8, 128), jnp.int32)
        for h in range(2):
            for d in range(narrow):
                for s in range(HALF):
                    at = (h * narrow + d) * CHUNK + s
                    lead = jnp.where(base == at, pair_ref[d * slot_count + c * CHUNK + h * HALF + s], lead)
        wave = jnp.where((lanes & HALF) == HALF, M - 1 - lead, lead).astype(jnp.float32)
        here = pl.ds(pl.multiple_of(c * 128, 128), 128)
        rows_of = jnp.broadcast_to(wave[:1], (FINE, 128))
        index = iota((FINE, 128), 0).astype(jnp.float32)
        cosine, sine = turn(rows_of * (index * (2.0 * FINE)))
        coarse[0, :, here] = cosine
        coarse[1, :, here] = sine
        cosine, sine = turn(rows_of * (index * 2.0 + 1.0))
        fine[0, :, here] = cosine
        fine[1, :, here] = sine
        down = jnp.transpose(jnp.broadcast_to(wave[:1], (128, 128)))
        cosine, sine = turn(down * (lon - 1.0))
        low = iota((128, 128), 1) < 64
        cosine = cosine * (M ** -0.5)
        sine = sine * (M ** -0.5)
        rate = down * (1.0 / M)
        coef[0, here, :] = cosine * jnp.where(low, 1.0, -rate)
        coef[1, here, :] = sine * jnp.where(low, -1.0, -rate)
        coef[2, here, :] = sine * jnp.where(low, 1.0, -rate)
        coef[3, here, :] = cosine * jnp.where(low, 1.0, rate)

    def one_chunk(c, carry):
        slot = lax.rem(c, 2)
        for copy in fetches(c, slot):
            copy.wait()

        @pl.when(c + 1 < chunks)
        def _():
            start_fetch(c + 1, 1 - slot)

        def widen(n, carry):
            part = table_buf[slot, pl.ds(n * block, block)].astype(jnp.float32)
            where_to = pl.ds(pl.multiple_of(n * block * pairs, 8), block * pairs)
            spread[where_to, :] = part.reshape(block * pairs, 128)
            return carry

        lax.fori_loop(0, 8, widen, 0)
        spread[M * pairs:, :] = table_buf[slot, M].astype(jnp.float32)

        def halves(h, carry):
            one_half(c, slot, h)
            return carry

        lax.fori_loop(0, 2, halves, 0)
        tables(c)
        return carry

    lax.fori_loop(0, chunks, one_chunk, 0)

    def turned(pieces, here):
        evens, odds = [], []
        c1, s1, c2, s2 = (coef[n, here, :] for n in range(4))
        for t in range(steps_here):
            data = jnp.concatenate([held[c, d, span, t * 128:(t + 1) * 128] for c, d, span in pieces], axis=0)
            other = pltpu.roll(data, 64, 1)
            evens.append(data * c1 + other * s1)
            odds.append(data * c2 + other * s2)
        return split(jnp.concatenate(evens, axis=1)), split(jnp.concatenate(odds, axis=1))

    def waves_at(g, coarse_of, fine_of):
        cosines, sines = [], []
        many = GROUP // FINE
        span = pl.ds(pl.multiple_of(g * many, many), many)
        cu, su = coarse_of(0, span), coarse_of(1, span)
        c2, s2 = fine_of
        for u in range(many):
            c1, s1 = cu[u:u + 1], su[u:u + 1]
            cosines.append(c1 * c2 - s1 * s2)
            sines.append(s1 * c2 + c1 * s2)
        return split(jnp.concatenate(cosines, axis=0)), split(jnp.concatenate(sines, axis=0))

    def span_of(h):
        return pl.ds(h * CHUNK, CHUNK)

    regions = wide * REG_DEV
    blocks = half_lon // 8

    def region_tables():
        number = iota((regions, 128), 0)
        begin = jnp.zeros((regions, 128), jnp.int32)
        end = begin
        for n in range(lon // 128):
            ids = region_ref[n:n + 1, :]
            begin = begin + jnp.where(ids < number, 1, 0)
            end = end + jnp.where(ids <= number, 1, 0)
        reach = 64
        while reach:
            begin = begin + pltpu.roll(begin, reach, 1)
            end = end + pltpu.roll(end, reach, 1)
            reach //= 2
        lanes = iota((regions, 128), 1)
        for side in range(2):
            if side == 0:
                first, last = half_lon - jnp.minimum(end, half_lon), half_lon - jnp.minimum(begin, half_lon)
            else:
                first, last = jnp.maximum(begin, half_lon) - half_lon, jnp.maximum(end, half_lon) - half_lon
            here = first < last
            for n in range(half_lon // 128):
                hit = (lanes + n * 128 == first) & here
                pick[side, :, n * 128:(n + 1) * 128] = jnp.where(hit, 1.0, 0.0).astype(jnp.bfloat16)
            start = (first + 7) >> 3
            whole = start * 8 < last
            pick_blocks[side] = jnp.where((lanes == start) & whole, 1.0, 0.0).astype(jnp.bfloat16)
            absent[2 * side] = jnp.where(here, 0.0, -1e30)
            absent[2 * side + 1] = jnp.where(whole, 0.0, -1e30)
        across, down = iota((128, 128), 1), iota((128, 128), 0)
        mirror = jnp.where(across + down == 127, 1.0, 0.0).astype(jnp.bfloat16)
        ids = region_ref[...].astype(jnp.float32)
        flipped = dot(ids.astype(jnp.bfloat16), mirror)
        tiles = half_lon // 128
        sub = iota((16, 8, 128), 1)
        for side in range(2):
            for n in range(tiles):
                source = flipped[tiles - 1 - n:tiles - n] if side == 0 else ids[tiles + n:tiles + n + 1]
                column = jnp.transpose(jnp.broadcast_to(source, (128, 128)))
                span = pl.ds(side * half_lon + n * 128, 128)
                field[span, :] = column
                column = column.reshape(16, 8, 128)
                for i, step in enumerate((1, 2, 4)):
                    same = (pltpu.roll(column, 8 - step, 1) == column) & (sub + step < 8)
                    apart[i, span, :] = jnp.where(same, 0.0, -1e30).reshape(128, 128)
            starts = field[pl.ds(side * half_lon, blocks, stride=8), :]
            for i, step in enumerate((1, 2, 4)):
                same = (pltpu.roll(starts, blocks - step, 0) == starts) & (iota((blocks, 128), 0) + step < blocks)
                apart_blocks[side, i] = jnp.where(same, 0.0, -1e30)

    region_tables()

    def arrive(c, h):
        for ahead in range(1, narrow):
            receive(c, ahead, h).wait_recv()

    def two_chunks(k, carry):
        first = 2 * k

        @pl.when(k == 0)
        def _():
            arrive(0, 0)
            arrive(0, 1)

        @pl.when(k > 0)
        def _():
            arrive(first, None)

        arrive(first + 1, None)
        here = pl.ds(pl.multiple_of(first * 128, 256), 256)
        pieces = [(first + n, d, span_of(h)) for n in range(2) for h in range(2) for d in range(narrow)]
        (even_hi, even_lo), (odd_hi, odd_lo) = turned(pieces, here)
        fine_of = fine[0, :, here], fine[1, :, here]

        def one_group(g, carry):
            (cos_hi, cos_lo), (sin_hi, sin_lo) = waves_at(g, lambda n, span: coarse[n, span, here], fine_of)
            where_to = pl.ds(pl.multiple_of(g * GROUP, GROUP), GROUP)
            new_cos = dot(cos_hi, even_hi) + dot(cos_lo, even_hi) + dot(cos_hi, even_lo)
            new_sin = dot(sin_hi, odd_hi) + dot(sin_lo, odd_hi) + dot(sin_hi, odd_lo)

            @pl.when(k == 0)
            def _():
                part_cos[where_to, :] = new_cos
                part_sin[where_to, :] = new_sin

            @pl.when(k > 0)
            def _():
                part_cos[where_to, :] += new_cos
                part_sin[where_to, :] += new_sin

            return carry

        lax.fori_loop(0, half_lon // GROUP, one_group, 0)
        return carry

    lax.fori_loop(0, chunks // 2 - 1, two_chunks, 0)

    def half_chunk(c, h, last):
        here = pl.ds((c * 2 + h) * 64, 64)
        (even_hi, even_lo), (odd_hi, odd_lo) = turned([(c, d, span_of(h)) for d in range(narrow)], here)
        even = jnp.concatenate([even_hi, even_hi, even_lo, jnp.zeros_like(even_lo)], axis=0)
        odd = jnp.concatenate([odd_hi, odd_hi, odd_lo, jnp.zeros_like(odd_lo)], axis=0)
        chunk_here = pl.ds(c * 128, 128)

        def doubled(values):
            kept = iota(values.shape, 1) < 64
            moved = pltpu.roll(values, 64, 1)
            return jnp.where(kept, values, moved) if h == 0 else jnp.where(kept, moved, values)

        fine_of = tuple(doubled(fine[n, :, chunk_here]) for n in range(2))
        low = iota((GROUP, 128), 1) < 64
        slopes = iota((GROUP, 128), 1) >= 64

        def one_group(g, carry):
            (cos_hi, cos_lo), (sin_hi, sin_lo) = waves_at(
                g, lambda n, span: doubled(coarse[n, span, chunk_here]), fine_of
            )
            where_to = pl.ds(pl.multiple_of(g * GROUP, GROUP), GROUP)
            new_cos = dot(jnp.concatenate([jnp.where(low, cos_hi, cos_lo), cos_hi], axis=1), even)
            new_sin = dot(jnp.concatenate([jnp.where(low, sin_hi, sin_lo), sin_hi], axis=1), odd)
            if not last:
                part_cos[where_to, :] += new_cos
                part_sin[where_to, :] += new_sin
                return carry
            most = [None, None]
            least = [None, None]
            for t in range(steps_here):
                lanes = slice(t * 128, (t + 1) * 128)
                even_part = part_cos[where_to, lanes] + new_cos[:, lanes]
                odd_part = part_sin[where_to, lanes] + new_sin[:, lanes]
                for side, full in enumerate((even_part + odd_part, even_part - odd_part)):
                    most[side] = full if t == 0 else jnp.maximum(most[side], full)
                    least[side] = full if t == 0 else jnp.minimum(least[side], full)
            for side in range(2):
                span = pl.ds(pl.multiple_of(side * half_lon + g * GROUP, GROUP), GROUP)
                best = jnp.maximum(most[side], jnp.where(slopes, -least[side], most[side]))
                best = best.reshape(GROUP // 8, 8, 128)
                for i, step in enumerate((1, 2, 4)):
                    best = jnp.maximum(
                        best, pltpu.roll(best, 8 - step, 1) + apart[i, span, :].reshape(GROUP // 8, 8, 128)
                    )
                field[span, :] = best.reshape(GROUP, 128)
            return carry

        lax.fori_loop(0, half_lon // GROUP, one_group, 0)

    arrive(chunks - 2, None)
    half_chunk(chunks - 2, 0, False)
    half_chunk(chunks - 2, 1, False)
    arrive(chunks - 1, 0)
    half_chunk(chunks - 1, 0, False)
    arrive(chunks - 1, 1)
    half_chunk(chunks - 1, 1, True)

    def chosen(picks, values, missing):
        high, low = split(values)
        both = dot(picks, jnp.concatenate([high, low], axis=1))
        return both[:, :128] + both[:, 128:] + missing

    parts = []
    for side in range(2):
        starts = field[pl.ds(side * half_lon, blocks, stride=8), :]
        for i, step in enumerate((1, 2, 4)):
            starts = jnp.maximum(starts, pltpu.roll(starts, blocks - step, 0) + apart_blocks[side, i])
        parts.append(chosen(pick_blocks[side], starts, absent[2 * side + 1]))
        parts.append(chosen(pick[side], field[pl.ds(side * half_lon, half_lon), :], absent[2 * side]))
    peaks[...] = jnp.maximum(jnp.maximum(parts[0], parts[1]), jnp.maximum(parts[2], parts[3]))

    def exchange(ahead, arriving):
        other = lax.rem(me_wide + ahead, wide)
        return pltpu.make_async_remote_copy(
            src_ref=peaks.at[pl.ds(pl.multiple_of(other * REG_DEV, REG_DEV), REG_DEV)],
            dst_ref=peaks_in.at[other if arriving else me_wide],
            send_sem=wide_send.at[other], recv_sem=wide_recv.at[other if arriving else me_wide],
            device_id={"wide": other}, device_id_type=MESH,
        )

    for ahead in range(wide - 1, 0, -1):
        exchange(ahead, False).start()
    best = peaks[pl.ds(pl.multiple_of(me_wide * REG_DEV, REG_DEV), REG_DEV), :]
    for ahead in range(1, wide):
        exchange(ahead, True).wait_recv()
        best = jnp.maximum(best, peaks_in[lax.rem(me_wide + ahead, wide)])
    for n in range(2 * members):
        out_ref[n] = best[:, n * lat_here:(n + 1) * lat_here]

    for ahead in range(1, wide):
        exchange(ahead, False).wait_send()
    for c in (0, chunks - 1):
        for h in range(2):
            for ahead in range(1, narrow):
                send(c, ahead, h).wait_send()

    def drain(c, carry):
        for ahead in range(1, narrow):
            send(c, ahead, None).wait_send()
        return carry

    lax.fori_loop(1, chunks - 1, drain, 0)


def per_device(spectra, legendre, pair_of_slot, lat_owner, region_of_lon):
    members, steps_here, slot_count, _, length = spectra.shape
    lat = legendre.shape[2]
    narrow, wide = lax.axis_size("narrow"), lax.axis_size("wide")
    lat_here = lat // narrow
    lon = region_of_lon.shape[0]
    rows = members * steps_here * 2
    chunks = slot_count // CHUNK
    regions = REG_DEV * wide
    lanes = steps_here * 128
    dims = (narrow, wide, chunks, rows, members, steps_here, lat_here, lon)
    vmem = pl.BlockSpec(memory_space=pltpu.VMEM)
    hbm = pl.BlockSpec(memory_space=pl.ANY)
    best = pl.pallas_call(
        functools.partial(fields_kernel, dims),
        in_specs=[pl.BlockSpec(memory_space=pltpu.SMEM), vmem, vmem, hbm, hbm],
        out_specs=vmem,
        out_shape=jax.ShapeDtypeStruct((2 * members, REG_DEV, lat_here), jnp.float32),
        scratch_shapes=[
            pltpu.VMEM((2, length, CHUNK // 2, lat), jnp.bfloat16),
            pltpu.VMEM((2, members, steps_here, CHUNK, 2, length), jnp.bfloat16),
            pltpu.VMEM((HALF, rows, length), jnp.float32),
            pltpu.VMEM((length * CHUNK // 2, 128), jnp.float32),
            pltpu.VMEM((CHUNK * rows, 128), jnp.float32),
            pltpu.VMEM((2 * members * lat, narrow * 128), jnp.bfloat16),
            pltpu.VMEM((chunks, narrow, 2 * CHUNK, lanes), jnp.float32),
            pltpu.VMEM((chunks, narrow, 2 * CHUNK, lanes), jnp.float32),
            pltpu.VMEM((4, chunks * 128, 128), jnp.float32),
            pltpu.VMEM((2, FINE, chunks * 128), jnp.float32),
            pltpu.VMEM((2, FINE, chunks * 128), jnp.float32),
            pltpu.VMEM((lon // 2, lanes), jnp.float32),
            pltpu.VMEM((lon // 2, lanes), jnp.float32),
            pltpu.VMEM((lon, 128), jnp.float32),
            pltpu.VMEM((3, lon, 128), jnp.float32),
            pltpu.VMEM((2, 3, lon // 16, 128), jnp.float32),
            pltpu.VMEM((2, regions, lon // 2), jnp.bfloat16),
            pltpu.VMEM((2, regions, lon // 16), jnp.bfloat16),
            pltpu.VMEM((4, regions, 128), jnp.float32),
            pltpu.VMEM((regions, 128), jnp.float32),
            pltpu.VMEM((wide, REG_DEV, 128), jnp.float32),
            pltpu.SemaphoreType.DMA((2, 2)),
            pltpu.SemaphoreType.DMA((2, chunks, narrow)),
            pltpu.SemaphoreType.DMA((2, chunks, narrow)),
            pltpu.SemaphoreType.DMA((wide,)),
            pltpu.SemaphoreType.DMA((wide,)),
        ],
        compiler_params=pltpu.CompilerParams(
            collective_id=0, has_side_effects=True, vmem_limit_bytes=60 * 1024 * 1024
        ),
    )(
        pair_of_slot, lat_owner.reshape(1, lat), region_of_lon.reshape(-1, 128), spectra,
        jnp.transpose(legendre, (1, 0, 2)),
    )
    best = jnp.transpose(best, (0, 2, 1))
    return (best[:members], best[members:])


def solution(mesh):
    in_specs = (
        P(None, ("groups", "wide"), "narrow", None, None),
        P("narrow", None, None),
        P(),
        P(),
        P(),
    )
    out_specs = (P("groups", "narrow", "wide"), P("groups", "narrow", "wide"))

    def body(spectra, legendre, *rest):
        members, steps_here, slot_count = spectra.shape[:3]
        lat_here = legendre.shape[2] // mesh.shape["narrow"]
        packs = steps_here * lat_here == 128 and 2 * members * lat_here == 128
        packs = packs and slot_count % (2 * CHUNK) == 0 and slot_count >= 4 * CHUNK
        packs = packs and legendre.shape[2] == 128 and mesh.shape["narrow"] * CHUNK == 64
        packs = packs and rest[2].shape[0] == 2 * FINE * FINE
        chosen = per_device if packs else per_device_plain
        return chosen(spectra, legendre, *rest)

    return jax.shard_map(
        body, mesh=mesh, in_specs=in_specs, out_specs=out_specs, check_vma=False
    )
```

profile of v0, /device:TPU:8, one launch (start us, length us, event | category | flops | bytes accessed | tf_op | source)
XLA Modules:
  0.0 76.4 jit_solution(7847330422252762712)
XLA Ops:
  0.6 74.4 %shard_map.68 = f32[4,16,32]{2,1,0:T(8,128)} custom-call(s32[640]{0:T(1024)} %pair_ref.1, s32[1,128]{1,0:T(1,128)} %bitcast.7, s32[16,128]{1,0:T(8,128)} %bitcast.6, bf16[2,4,160,2,1281]{4,3,2,1,0:T(2,128)(2,1)} %x_hbm.1, bf16[1281,80,128]{2,1,0:T(8,128)(2,1)} %bitcast.4), custom_call_target="tpu_custom_call" | custom-call | tf_op jit(solution)/shard_map/pallas_call | solution.py:607
  75.1 1.3 %fusion = (f32[2,32,16]{1,2,0:T(8,128)}, f32[2,32,16]{1,2,0:T(8,128)}) fusion(f32[4,32,16]{1,2,0:T(8,128)} %bitcast.5), kind=kLoop, calls=%fused_computation | loop fusion | bytes 16384 | tf_op jit(solution)/shard_map/slice | solution.py:648
where the time goes:
time: 77.8 us; the launch traced here: 76.4 us
  Pallas kernels  74.4 us (96%)
  local copies, waits for them, and re-layouts  1.35 us (2%)
    pallas_call x1, Pallas kernels, per_device(): pl.pallas_call(functools.partial(fields_kernel, dims), in_specs=[pl.Block...  74.4 us

commit v1 on v0

--- a/solution.py
+++ b/solution.py
@@ -102,6 +102,9 @@
 HALF = 8
 FINE = 32
 GROUP = 256
+FETCHES = 4
+LAST = 512
+WIDEN = 32
 MESH = pl.DeviceIdType.MESH
 
 
@@ -137,7 +140,7 @@
 
 def fields_kernel(
     dims, pair_ref, owner_ref, region_ref, x_hbm, table_hbm, out_ref,
-    table_buf, x_buf, lined, spread, sums, place, sent, held, coef, coarse, fine, part_cos, part_sin, field,
+    table_buf, x_buf, lined, spread, last_row, sums, place, sent, held, ready, coef, coarse, fine, part_cos, part_sin, field,
     apart, apart_blocks, pick, pick_blocks, absent, peaks, peaks_in,
     fetch_sem, send_sem, recv_sem, wide_send, wide_recv,
 ):
@@ -149,14 +152,20 @@
     half_lon = lon // 2
     lat = narrow * lat_here
 
+    part = M // FETCHES
+    parts_of = [pl.ds(n * part, part + (n == FETCHES - 1)) for n in range(FETCHES)]
+
     def fetches(c, slot):
         return (
-            pltpu.make_async_copy(
-                table_hbm.at[:, pl.ds(pl.multiple_of(c * pairs, pairs), pairs), :], table_buf.at[slot],
-                fetch_sem.at[0, slot],
+            *(
+                pltpu.make_async_copy(
+                    table_hbm.at[span, pl.ds(pl.multiple_of(c * pairs, pairs), pairs), :], table_buf.at[slot, span],
+                    fetch_sem.at[1 + n, slot],
+                )
+                for n, span in enumerate(parts_of)
             ),
             pltpu.make_async_copy(
-                x_hbm.at[:, :, pl.ds(c * CHUNK, CHUNK), :, :], x_buf.at[slot], fetch_sem.at[1, slot]
+                x_hbm.at[:, :, pl.ds(c * CHUNK, CHUNK), :, :], x_buf.at[slot], fetch_sem.at[0, slot]
             ),
         )
 
@@ -169,25 +178,29 @@
 
     order = (2, 1, 3) if narrow == 4 else tuple(range(1, narrow))
 
-    def send(c, ahead, h):
+    def rows_of(c, kind):
+        if kind < 2:
+            return pl.ds(pl.multiple_of(c * 2 * CHUNK + kind * CHUNK, CHUNK), CHUNK), kind
+        return pl.ds(pl.multiple_of(c * 2 * CHUNK, 2 * CHUNK), (kind - 1) * 2 * CHUNK), 0
+
+    def send(c, ahead, kind):
         target = partner(ahead)
-        span = pl.ds(0, 2 * CHUNK) if h is None else pl.ds(h * CHUNK, CHUNK)
-        at = 0 if h is None else h
+        span, at = rows_of(c, kind)
         return pltpu.make_async_remote_copy(
-            src_ref=sent.at[c, target, span], dst_ref=held.at[c, me, span],
+            src_ref=sent.at[target, span], dst_ref=held.at[me, span],
             send_sem=send_sem.at[at, c, target], recv_sem=recv_sem.at[at, c, me],
             device_id={"narrow": target}, device_id_type=MESH,
         )
 
-    def receive(c, ahead, h):
-        origin = partner(ahead)
-        span = pl.ds(0, 2 * CHUNK) if h is None else pl.ds(h * CHUNK, CHUNK)
-        at = 0 if h is None else h
-        return pltpu.make_async_remote_copy(
-            src_ref=sent.at[c, origin, span], dst_ref=held.at[c, origin, span],
-            send_sem=send_sem.at[at, c, origin], recv_sem=recv_sem.at[at, c, origin],
-            device_id={"narrow": origin}, device_id_type=MESH,
-        )
+    def arrive(c, kind):
+        for ahead in range(1, narrow):
+            origin = partner(ahead)
+            span, at = rows_of(c, kind)
+            pltpu.make_async_remote_copy(
+                src_ref=sent.at[origin, span], dst_ref=held.at[origin, span],
+                send_sem=send_sem.at[at, c, origin], recv_sem=recv_sem.at[at, c, origin],
+                device_id={"narrow": origin}, device_id_type=MESH,
+            ).wait_recv()
 
     start_fetch(0, 0)
     barrier = pltpu.get_barrier_semaphore()
@@ -212,39 +225,39 @@
         place[n * lat:(n + 1) * lat, :] = jnp.where(wanted, 1.0, 0.0).astype(jnp.bfloat16)
 
     position = iota((1, M), 1)
+    sign = (1 - 2 * (position & 1)).astype(jnp.float32).astype(jnp.bfloat16)
     half_lane = iota((rows, 128), 1)
     block = M // 8
 
-    def one_pair(c, slot, at, u):
+    def one_pair(c, slot, h, u):
+        at = h * (HALF // 2) + u
         parts = []
         extras = []
         for half in range(2):
             inside = 2 * at + half
             lines = 2 * u + half
             first_len = M - pair_ref[me * slot_count + c * CHUNK + inside]
-            leading = (position < first_len).astype(jnp.float32)
-            trailing = 1.0 - leading
-            sign_lead = (1 - 2 * (position & 1)).astype(jnp.float32)
+            leading = (position < first_len).astype(jnp.float32).astype(jnp.bfloat16)
             flip = (1 - 2 * (first_len & 1)).astype(jnp.float32)
             for e in range(members):
                 for t in range(steps_here):
                     row = 2 * (e * steps_here + t)
-                    lined[lines, row:row + 2, :] = x_buf[slot, e, t, inside].astype(jnp.float32)
-            body = lined[lines, :, :M].astype(jnp.bfloat16)
-            for mask in (leading, leading * sign_lead, trailing, trailing * (sign_lead * flip)):
-                parts.append(body * mask.astype(jnp.bfloat16))
-            last = lined[lines, :, M:]
+                    lined[lines, row:row + 2, :] = x_buf[slot, e, t, inside]
+            body = lined[lines, :, :M]
+            first_part = body * leading
+            parts.extend((first_part, first_part * sign, body, body * sign))
+            last = lined[lines, :, M:].astype(jnp.float32)
             extras.append((last, flip))
-        table = spread[pl.ds(at, M, stride=pairs), :].astype(jnp.bfloat16)
+        table = spread[h, pl.ds(u, M, stride=4), :].astype(jnp.bfloat16)
         out = dot(jnp.concatenate(parts, axis=0), table)
-        edge = spread[pl.ds(M * pairs + at, 1), :]
+        edge = last_row[pl.ds(at, 1), :]
         for half in range(2):
             base = half * 4 * rows
             piece = [out[base + v * rows:base + (v + 1) * rows] for v in range(4)]
             last, flip = extras[half]
             term = last * edge
-            piece[2] = piece[2] + term
-            piece[3] = piece[3] + term * flip
+            piece[2] = piece[2] - piece[0] + term
+            piece[3] = (piece[3] - piece[1] + term) * flip
             for tail_at in range(2):
                 north, south = piece[2 * tail_at], piece[2 * tail_at + 1]
                 if half == 0:
@@ -256,7 +269,7 @@
 
     def one_half(c, slot, h):
         for u in range(HALF // 2):
-            one_pair(c, slot, h * (HALF // 2) + u, u)
+            one_pair(c, slot, h, u)
         highs, lows = [], []
         for t in range(steps_here):
             wide_rows = jnp.concatenate(
@@ -271,39 +284,30 @@
             lows.append(low)
         both = dot(jnp.concatenate(highs + lows, axis=0), place[...])
         moved = both[:steps_here * CHUNK] + both[steps_here * CHUNK:]
-        where_to = pl.ds(pl.multiple_of(h * CHUNK, CHUNK), CHUNK)
+        where_to = pl.ds(pl.multiple_of((2 * c + h) * CHUNK, CHUNK), CHUNK)
         for t in range(steps_here):
             for d in range(narrow):
-                sent[c, d, where_to, t * 128:(t + 1) * 128] = (
+                sent[d, where_to, t * 128:(t + 1) * 128] = (
                     moved[t * CHUNK:(t + 1) * CHUNK, d * 128:(d + 1) * 128]
                 )
-        held[c, me, where_to, :] = sent[c, me, where_to, :]
+        held[me, where_to, :] = sent[me, where_to, :]
+
+        def send_when(when, first, kind):
+            @pl.when(when)
+            def _():
+                for ahead in order:
+                    send(first, ahead, kind).start()
 
         @pl.when((c == 0) & (h == 0))
         def _():
             pl.semaphore_wait(barrier, narrow - 1 + wide - 1)
-            for ahead in order:
-                send(0, ahead, 0).start()
-
-        @pl.when((c == 0) & (h == 1))
-        def _():
-            for ahead in order:
-                send(0, ahead, 1).start()
-
-        @pl.when((c == chunks - 1) & (h == 0))
-        def _():
-            for ahead in order:
-                send(chunks - 1, ahead, 0).start()
-
-        @pl.when((c == chunks - 1) & (h == 1))
-        def _():
-            for ahead in order:
-                send(chunks - 1, ahead, 1).start()
-
-        @pl.when((c > 0) & (c < chunks - 1) & (h == 1))
-        def _():
-            for ahead in order:
-                send(c, ahead, None).start()
+
+        send_when((c == 0) & (h == 0), 0, 0)
+        send_when((c == 0) & (h == 1), 0, 1)
+        send_when(((c == 1) | (c == chunks - 2)) & (h == 1), c, 2)
+        send_when((c > 1) & (c < chunks - 2) & (lax.rem(c, 2) == 1) & (h == 1), c - 1, 3)
+        send_when((c == chunks - 1) & (h == 0), chunks - 1, 0)
+        send_when((c == chunks - 1) & (h == 1), chunks - 1, 1)
 
     def tables(c):
         lanes = iota((8, 128), 1)
@@ -344,16 +348,39 @@
         def _():
             start_fetch(c + 1, 1 - slot)
 
-        def widen(n, carry):
-            part = table_buf[slot, pl.ds(n * block, block)].astype(jnp.float32)
-            where_to = pl.ds(pl.multiple_of(n * block * pairs, 8), block * pairs)
-            spread[where_to, :] = part.reshape(block * pairs, 128)
-            return carry
-
-        lax.fori_loop(0, 8, widen, 0)
-        spread[M * pairs:, :] = table_buf[slot, M].astype(jnp.float32)
+        def widen(groups):
+            def some(n, carry):
+                for v in range(block // WIDEN):
+                    at = n * block + v * WIDEN
+                    part = table_buf[slot, pl.ds(at, WIDEN)].astype(jnp.float32).reshape(WIDEN // 2, 2, pairs, 128)
+                    first, second = part[:, 0], part[:, 1]
+                    upper = iota(first.shape, 1) < 4
+                    where_to = pl.ds(pl.multiple_of(at * 4, 8), WIDEN * 4)
+                    if 0 in groups:
+                        merged = jnp.where(upper, first, pltpu.roll(second, 4, 1))
+                        spread[0, where_to, :] = merged.reshape(WIDEN * 4, 128)
+                    if 1 in groups:
+                        merged = jnp.where(upper, pltpu.roll(first, 4, 1), second)
+                        spread[1, where_to, :] = merged.reshape(WIDEN * 4, 128)
+                return carry
+
+            lax.fori_loop(0, 8, some, 0)
+
+        @pl.when(c > 0)
+        def _():
+            widen((0, 1))
+
+        last_row[...] = table_buf[slot, M].astype(jnp.float32)
 
         def halves(h, carry):
+            @pl.when((c == 0) & (h == 0))
+            def _():
+                widen((0,))
+
+            @pl.when((c == 0) & (h == 1))
+            def _():
+                widen((1,))
+
             one_half(c, slot, h)
             return carry
 
@@ -367,7 +394,7 @@
         evens, odds = [], []
         c1, s1, c2, s2 = (coef[n, here, :] for n in range(4))
         for t in range(steps_here):
-            data = jnp.concatenate([held[c, d, span, t * 128:(t + 1) * 128] for c, d, span in pieces], axis=0)
+            data = jnp.concatenate([held[d, span, t * 128:(t + 1) * 128] for d, span in pieces], axis=0)
             other = pltpu.roll(data, 64, 1)
             evens.append(data * c1 + other * s1)
             odds.append(data * c2 + other * s2)
@@ -385,8 +412,8 @@
             sines.append(s1 * c2 + c1 * s2)
         return split(jnp.concatenate(cosines, axis=0)), split(jnp.concatenate(sines, axis=0))
 
-    def span_of(h):
-        return pl.ds(h * CHUNK, CHUNK)
+    def span_of(c, h):
+        return pl.ds(pl.multiple_of((2 * c + h) * CHUNK, CHUNK), CHUNK)
 
     regions = wide * REG_DEV
     blocks = half_lon // 8
@@ -442,10 +469,6 @@
 
     region_tables()
 
-    def arrive(c, h):
-        for ahead in range(1, narrow):
-            receive(c, ahead, h).wait_recv()
-
     def two_chunks(k, carry):
         first = 2 * k
 
@@ -453,14 +476,14 @@
         def _():
             arrive(0, 0)
             arrive(0, 1)
+            arrive(1, 2)
 
         @pl.when(k > 0)
         def _():
-            arrive(first, None)
-
-        arrive(first + 1, None)
+            arrive(first, 3)
+
         here = pl.ds(pl.multiple_of(first * 128, 256), 256)
-        pieces = [(first + n, d, span_of(h)) for n in range(2) for h in range(2) for d in range(narrow)]
+        pieces = [(d, span_of(first + n, h)) for n in range(2) for h in range(2) for d in range(narrow)]
         (even_hi, even_lo), (odd_hi, odd_lo) = turned(pieces, here)
         fine_of = fine[0, :, here], fine[1, :, here]
 
@@ -487,11 +510,7 @@
 
     lax.fori_loop(0, chunks // 2 - 1, two_chunks, 0)
 
-    def half_chunk(c, h, last):
-        here = pl.ds((c * 2 + h) * 64, 64)
-        (even_hi, even_lo), (odd_hi, odd_lo) = turned([(c, d, span_of(h)) for d in range(narrow)], here)
-        even = jnp.concatenate([even_hi, even_hi, even_lo, jnp.zeros_like(even_lo)], axis=0)
-        odd = jnp.concatenate([odd_hi, odd_hi, odd_lo, jnp.zeros_like(odd_lo)], axis=0)
+    def angles_ahead(c, h):
         chunk_here = pl.ds(c * 128, 128)
 
         def doubled(values):
@@ -501,15 +520,28 @@
 
         fine_of = tuple(doubled(fine[n, :, chunk_here]) for n in range(2))
         low = iota((GROUP, 128), 1) < 64
-        slopes = iota((GROUP, 128), 1) >= 64
 
         def one_group(g, carry):
-            (cos_hi, cos_lo), (sin_hi, sin_lo) = waves_at(
-                g, lambda n, span: doubled(coarse[n, span, chunk_here]), fine_of
-            )
+            both = waves_at(g, lambda n, span: doubled(coarse[n, span, chunk_here]), fine_of)
             where_to = pl.ds(pl.multiple_of(g * GROUP, GROUP), GROUP)
-            new_cos = dot(jnp.concatenate([jnp.where(low, cos_hi, cos_lo), cos_hi], axis=1), even)
-            new_sin = dot(jnp.concatenate([jnp.where(low, sin_hi, sin_lo), sin_hi], axis=1), odd)
+            for n, (high, part) in enumerate(both):
+                ready[h, n, where_to, :128] = jnp.where(low, high, part)
+                ready[h, n, where_to, 128:] = high
+            return carry
+
+        lax.fori_loop(0, half_lon // GROUP, one_group, 0)
+
+    def half_chunk(c, h, last):
+        here = pl.ds((c * 2 + h) * 64, 64)
+        (even_hi, even_lo), (odd_hi, odd_lo) = turned([(d, span_of(c, h)) for d in range(narrow)], here)
+        even = jnp.concatenate([even_hi, even_hi, even_lo, jnp.zeros_like(even_lo)], axis=0)
+        odd = jnp.concatenate([odd_hi, odd_hi, odd_lo, jnp.zeros_like(odd_lo)], axis=0)
+        sign = jnp.where(iota((LAST, 128), 1) < 64, 1.0, -1.0)
+
+        def one_group(g, carry):
+            where_to = pl.ds(pl.multiple_of(g * LAST, LAST), LAST)
+            new_cos = dot(ready[h, 0, where_to, :], even)
+            new_sin = dot(ready[h, 1, where_to, :], odd)
             if not last:
                 part_cos[where_to, :] += new_cos
                 part_sin[where_to, :] += new_sin
@@ -524,21 +556,25 @@
                     most[side] = full if t == 0 else jnp.maximum(most[side], full)
                     least[side] = full if t == 0 else jnp.minimum(least[side], full)
             for side in range(2):
-                span = pl.ds(pl.multiple_of(side * half_lon + g * GROUP, GROUP), GROUP)
-                best = jnp.maximum(most[side], jnp.where(slopes, -least[side], most[side]))
-                best = best.reshape(GROUP // 8, 8, 128)
+                span = pl.ds(pl.multiple_of(side * half_lon + g * LAST, LAST), LAST)
+                best = jnp.maximum(most[side], least[side] * sign)
+                best = best.reshape(LAST // 8, 8, 128)
                 for i, step in enumerate((1, 2, 4)):
                     best = jnp.maximum(
-                        best, pltpu.roll(best, 8 - step, 1) + apart[i, span, :].reshape(GROUP // 8, 8, 128)
+                        best, pltpu.roll(best, 8 - step, 1) + apart[i, span, :].reshape(LAST // 8, 8, 128)
                     )
-                field[span, :] = best.reshape(GROUP, 128)
+                field[span, :] = best.reshape(LAST, 128)
             return carry
 
-        lax.fori_loop(0, half_lon // GROUP, one_group, 0)
-
-    arrive(chunks - 2, None)
+        lax.fori_loop(0, half_lon // LAST, one_group, 0)
+
+    angles_ahead(chunks - 2, 0)
+    angles_ahead(chunks - 2, 1)
+    arrive(chunks - 2, 2)
     half_chunk(chunks - 2, 0, False)
     half_chunk(chunks - 2, 1, False)
+    angles_ahead(chunks - 1, 0)
+    angles_ahead(chunks - 1, 1)
     arrive(chunks - 1, 0)
     half_chunk(chunks - 1, 0, False)
     arrive(chunks - 1, 1)
@@ -569,6 +605,14 @@
 
     for ahead in range(wide - 1, 0, -1):
         exchange(ahead, False).start()
+    for ahead in range(1, narrow):
+        for kind in range(2):
+            send(0, ahead, kind).wait_send()
+            send(chunks - 1, ahead, kind).wait_send()
+        send(1, ahead, 2).wait_send()
+        send(chunks - 2, ahead, 2).wait_send()
+        for c in range(2, chunks - 2, 2):
+            send(c, ahead, 3).wait_send()
     best = peaks[pl.ds(pl.multiple_of(me_wide * REG_DEV, REG_DEV), REG_DEV), :]
     for ahead in range(1, wide):
         exchange(ahead, True).wait_recv()
@@ -578,17 +622,6 @@
 
     for ahead in range(1, wide):
         exchange(ahead, False).wait_send()
-    for c in (0, chunks - 1):
-        for h in range(2):
-            for ahead in range(1, narrow):
-                send(c, ahead, h).wait_send()
-
-    def drain(c, carry):
-        for ahead in range(1, narrow):
-            send(c, ahead, None).wait_send()
-        return carry
-
-    lax.fori_loop(1, chunks - 1, drain, 0)
 
 
 def per_device(spectra, legendre, pair_of_slot, lat_owner, region_of_lon):
@@ -612,12 +645,14 @@
         scratch_shapes=[
             pltpu.VMEM((2, length, CHUNK // 2, lat), jnp.bfloat16),
             pltpu.VMEM((2, members, steps_here, CHUNK, 2, length), jnp.bfloat16),
-            pltpu.VMEM((HALF, rows, length), jnp.float32),
-            pltpu.VMEM((length * CHUNK // 2, 128), jnp.float32),
+            pltpu.VMEM((HALF, rows, length), jnp.bfloat16),
+            pltpu.VMEM((2, M * 4, 128), jnp.float32),
+            pltpu.VMEM((CHUNK // 2, 128), jnp.float32),
             pltpu.VMEM((CHUNK * rows, 128), jnp.float32),
             pltpu.VMEM((2 * members * lat, narrow * 128), jnp.bfloat16),
-            pltpu.VMEM((chunks, narrow, 2 * CHUNK, lanes), jnp.float32),
-            pltpu.VMEM((chunks, narrow, 2 * CHUNK, lanes), jnp.float32),
+            pltpu.VMEM((narrow, chunks * 2 * CHUNK, lanes), jnp.float32),
+            pltpu.VMEM((narrow, chunks * 2 * CHUNK, lanes), jnp.float32),
+            pltpu.VMEM((2, 2, lon // 2, 256), jnp.bfloat16),
             pltpu.VMEM((4, chunks * 128, 128), jnp.float32),
             pltpu.VMEM((2, FINE, chunks * 128), jnp.float32),
             pltpu.VMEM((2, FINE, chunks * 128), jnp.float32),
@@ -631,7 +666,7 @@
             pltpu.VMEM((4, regions, 128), jnp.float32),
             pltpu.VMEM((regions, 128), jnp.float32),
             pltpu.VMEM((wide, REG_DEV, 128), jnp.float32),
-            pltpu.SemaphoreType.DMA((2, 2)),
+            pltpu.SemaphoreType.DMA((1 + FETCHES, 2)),
             pltpu.SemaphoreType.DMA((2, chunks, narrow)),
             pltpu.SemaphoreType.DMA((2, chunks, narrow)),
             pltpu.SemaphoreType.DMA((wide,)),

time: 77.8 us -> 76.5 us (0.983); the launches traced: 76.4 us -> 76.2 us
  no operation moved by 1% of the time
where the time goes in v1:
time: 76.5 us; the launch traced here: 76.2 us
  Pallas kernels  74.2 us (97%)
  local copies, waits for them, and re-layouts  1.35 us (2%)
    pallas_call x1, Pallas kernels, per_device(): pl.pallas_call(functools.partial(fields_kernel, dims), in_specs=[pl.Block...  74.2 us

profile of v1, /device:TPU:8, one launch (start us, length us, event | category | flops | bytes accessed | tf_op | source)
XLA Modules:
  0.0 76.2 jit_solution(9028383588797315471)
XLA Ops:
  0.6 74.2 %shard_map.68 = f32[4,16,32]{2,1,0:T(8,128)} custom-call(s32[640]{0:T(1024)} %pair_ref.1, s32[1,128]{1,0:T(1,128)} %bitcast.7, s32[16,128]{1,0:T(8,128)} %bitcast.6, bf16[2,4,160,2,1281]{4,3,2,1,0:T(2,128)(2,1)} %x_hbm.1, bf16[1281,80,128]{2,1,0:T(8,128)(2,1)} %bitcast.4), custom_call_target="tpu_custom_call" | custom-call | tf_op jit(solution)/shard_map/pallas_call | solution.py:640
  74.9 1.3 %fusion = (f32[2,32,16]{1,2,0:T(8,128)}, f32[2,32,16]{1,2,0:T(8,128)}) fusion(f32[4,32,16]{1,2,0:T(8,128)} %bitcast.5), kind=kLoop, calls=%fused_computation | loop fusion | bytes 16384 | tf_op jit(solution)/shard_map/slice | solution.py:683

commit v2 on v1

--- a/solution.py
+++ b/solution.py
@@ -138,11 +138,18 @@
     return lax.broadcasted_iota(jnp.int32, shape, dim)
 
 
+def pieces_of(chunks):
+    pieces = [(0, 0), (0, 1), (1, 2)]
+    pieces += [(c, 3) for c in range(2, chunks - 2, 2)]
+    return pieces + [(chunks - 2, 2), (chunks - 1, 0), (chunks - 1, 1)]
+
+
 def fields_kernel(
-    dims, pair_ref, owner_ref, region_ref, x_hbm, table_hbm, out_ref,
+    dims, pair_hbm, owner_hbm, region_hbm, x_hbm, table_hbm, out_ref,
+    pair_ref, owner_ref, region_ref,
     table_buf, x_buf, lined, spread, last_row, sums, place, sent, held, ready, coef, coarse, fine, part_cos, part_sin, field,
     apart, apart_blocks, pick, pick_blocks, absent, peaks, peaks_in,
-    fetch_sem, send_sem, recv_sem, wide_send, wide_recv,
+    fetch_sem, small_sem, send_sem, recv_sem, wide_send, wide_recv,
 ):
     narrow, wide, chunks, rows, members, steps_here, lat_here, lon = dims
     me = lax.axis_index("narrow")
@@ -169,6 +176,8 @@
             ),
         )
 
+    PIECES = pieces_of(chunks)
+
     def start_fetch(c, slot):
         for copy in fetches(c, slot):
             copy.start()
@@ -203,6 +212,14 @@
             ).wait_recv()
 
     start_fetch(0, 0)
+    small = [
+        pltpu.make_async_copy(source, goal, small_sem.at[n])
+        for n, (source, goal) in enumerate(
+            ((owner_hbm, owner_ref), (pair_hbm, pair_ref), (region_hbm, region_ref))
+        )
+    ]
+    for copy in small:
+        copy.start()
     barrier = pltpu.get_barrier_semaphore()
     for ahead in range(1, narrow):
         pl.semaphore_signal(barrier, inc=1, device_id={"narrow": partner(ahead)}, device_id_type=MESH)
@@ -210,6 +227,9 @@
         pl.semaphore_signal(
             barrier, inc=1, device_id={"wide": lax.rem(me_wide + ahead, wide)}, device_id_type=MESH
         )
+
+    for copy in small:
+        copy.wait()
 
     lane = iota((lat, lat), 1)
     below = iota((lat, lat), 0)
@@ -302,12 +322,9 @@
         def _():
             pl.semaphore_wait(barrier, narrow - 1 + wide - 1)
 
-        send_when((c == 0) & (h == 0), 0, 0)
-        send_when((c == 0) & (h == 1), 0, 1)
-        send_when(((c == 1) | (c == chunks - 2)) & (h == 1), c, 2)
-        send_when((c > 1) & (c < chunks - 2) & (lax.rem(c, 2) == 1) & (h == 1), c - 1, 3)
-        send_when((c == chunks - 1) & (h == 0), chunks - 1, 0)
-        send_when((c == chunks - 1) & (h == 1), chunks - 1, 1)
+        for first, kind in PIECES:
+            after = first + (kind == 3)
+            send_when((c == first) & (h == 0) if kind == 0 else (c == after) & (h == 1), first, kind)
 
     def tables(c):
         lanes = iota((8, 128), 1)
@@ -341,14 +358,20 @@
 
     def one_chunk(c, carry):
         slot = lax.rem(c, 2)
-        for copy in fetches(c, slot):
-            copy.wait()
-
-        @pl.when(c + 1 < chunks)
+        x_copy, *table_copies = reversed(fetches(c, slot))
+        x_copy.wait()
+        table_copies = table_copies[::-1]
+
+        @pl.when(c > 0)
         def _():
-            start_fetch(c + 1, 1 - slot)
-
-        def widen(groups):
+            for copy in table_copies:
+                copy.wait()
+
+            @pl.when(c + 1 < chunks)
+            def _():
+                start_fetch(c + 1, 1 - slot)
+
+        def widen(groups, arriving=()):
             def some(n, carry):
                 for v in range(block // WIDEN):
                     at = n * block + v * WIDEN
@@ -364,18 +387,26 @@
                         spread[1, where_to, :] = merged.reshape(WIDEN * 4, 128)
                 return carry
 
-            lax.fori_loop(0, 8, some, 0)
+            if not arriving:
+                lax.fori_loop(0, 8, some, 0)
+            each = 8 // max(len(arriving), 1)
+            for n, copy in enumerate(arriving):
+                copy.wait()
+                lax.fori_loop(n * each, (n + 1) * each, some, 0)
 
         @pl.when(c > 0)
         def _():
             widen((0, 1))
 
-        last_row[...] = table_buf[slot, M].astype(jnp.float32)
-
         def halves(h, carry):
             @pl.when((c == 0) & (h == 0))
             def _():
-                widen((0,))
+                widen((0,), table_copies)
+                start_fetch(1, 1)
+
+            @pl.when(h == 0)
+            def _():
+                last_row[...] = table_buf[slot, M].astype(jnp.float32)
 
             @pl.when((c == 0) & (h == 1))
             def _():
@@ -472,15 +503,14 @@
     def two_chunks(k, carry):
         first = 2 * k
 
-        @pl.when(k == 0)
-        def _():
-            arrive(0, 0)
-            arrive(0, 1)
-            arrive(1, 2)
-
-        @pl.when(k > 0)
-        def _():
-            arrive(first, 3)
+        def arrive_when(when, piece):
+            @pl.when(when)
+            def _():
+                arrive(*piece)
+
+        for piece in PIECES:
+            if piece[0] < chunks - 2:
+                arrive_when(k == piece[0] // 2, piece)
 
         here = pl.ds(pl.multiple_of(first * 128, 256), 256)
         pieces = [(d, span_of(first + n, h)) for n in range(2) for h in range(2) for d in range(narrow)]
@@ -570,7 +600,9 @@
 
     angles_ahead(chunks - 2, 0)
     angles_ahead(chunks - 2, 1)
-    arrive(chunks - 2, 2)
+    for piece in PIECES:
+        if piece[0] == chunks - 2:
+            arrive(*piece)
     half_chunk(chunks - 2, 0, False)
     half_chunk(chunks - 2, 1, False)
     angles_ahead(chunks - 1, 0)
@@ -606,13 +638,8 @@
     for ahead in range(wide - 1, 0, -1):
         exchange(ahead, False).start()
     for ahead in range(1, narrow):
-        for kind in range(2):
-            send(0, ahead, kind).wait_send()
-            send(chunks - 1, ahead, kind).wait_send()
-        send(1, ahead, 2).wait_send()
-        send(chunks - 2, ahead, 2).wait_send()
-        for c in range(2, chunks - 2, 2):
-            send(c, ahead, 3).wait_send()
+        for first, kind in PIECES:
+            send(first, ahead, kind).wait_send()
     best = peaks[pl.ds(pl.multiple_of(me_wide * REG_DEV, REG_DEV), REG_DEV), :]
     for ahead in range(1, wide):
         exchange(ahead, True).wait_recv()
@@ -639,10 +666,13 @@
     hbm = pl.BlockSpec(memory_space=pl.ANY)
     best = pl.pallas_call(
         functools.partial(fields_kernel, dims),
-        in_specs=[pl.BlockSpec(memory_space=pltpu.SMEM), vmem, vmem, hbm, hbm],
+        in_specs=[hbm] * 5,
         out_specs=vmem,
         out_shape=jax.ShapeDtypeStruct((2 * members, REG_DEV, lat_here), jnp.float32),
         scratch_shapes=[
+            pltpu.SMEM((slot_count * narrow,), jnp.int32),
+            pltpu.VMEM((1, lat), jnp.int32),
+            pltpu.VMEM((lon // 128, 128), jnp.int32),
             pltpu.VMEM((2, length, CHUNK // 2, lat), jnp.bfloat16),
             pltpu.VMEM((2, members, steps_here, CHUNK, 2, length), jnp.bfloat16),
             pltpu.VMEM((HALF, rows, length), jnp.bfloat16),
@@ -667,6 +697,7 @@
             pltpu.VMEM((regions, 128), jnp.float32),
             pltpu.VMEM((wide, REG_DEV, 128), jnp.float32),
             pltpu.SemaphoreType.DMA((1 + FETCHES, 2)),
+            pltpu.SemaphoreType.DMA((3,)),
             pltpu.SemaphoreType.DMA((2, chunks, narrow)),
             pltpu.SemaphoreType.DMA((2, chunks, narrow)),
             pltpu.SemaphoreType.DMA((wide,)),

time: 76.5 us -> 75.6 us (0.988)
  Pallas kernels: 74.2 us -> 73.3 us
    pallas_call x1, Pallas kernels: 74.2 us -> 73.3 us  [per_device(): pl.pallas_call(functools.partial(fields_kernel, dims), in_specs=[hbm] * 5...]
where the time goes in v2:
time: 75.6 us; the launch traced here: 75.3 us
  Pallas kernels  73.3 us (97%)
  local copies, waits for them, and re-layouts  1.35 us (2%)
    pallas_call x1, Pallas kernels, per_device(): pl.pallas_call(functools.partial(fields_kernel, dims), in_specs=[hbm] * 5...  73.3 us

profile of v2, /device:TPU:8, one launch (start us, length us, event | category | flops | bytes accessed | tf_op | source)
XLA Modules:
  0.0 75.3 jit_solution(13490818989506449902)
XLA Ops:
  0.6 73.3 %shard_map.68 = f32[4,16,32]{2,1,0:T(8,128)} custom-call(s32[640]{0:T(1024)} %pair_hbm.1, s32[1,128]{1,0:T(1,128)} %bitcast.7, s32[16,128]{1,0:T(8,128)} %bitcast.6, bf16[2,4,160,2,1281]{4,3,2,1,0:T(2,128)(2,1)} %x_hbm.1, bf16[1281,80,128]{2,1,0:T(8,128)(2,1)} %bitcast.4), custom_call_target="tpu_custom_call" | custom-call | tf_op jit(solution)/shard_map/pallas_call | solution.py:667
  74.0 1.3 %fusion = (f32[2,32,16]{1,2,0:T(8,128)}, f32[2,32,16]{1,2,0:T(8,128)}) fusion(f32[4,32,16]{1,2,0:T(8,128)} %bitcast.5), kind=kLoop, calls=%fused_computation | loop fusion | bytes 16384 | tf_op jit(solution)/shard_map/slice | solution.py:714

commit v3 on v2

--- a/solution.py
+++ b/solution.py
@@ -101,7 +101,7 @@
 CHUNK = 16
 HALF = 8
 FINE = 32
-GROUP = 256
+GROUP = 512
 FETCHES = 4
 LAST = 512
 WIDEN = 32
@@ -192,8 +192,7 @@
             return pl.ds(pl.multiple_of(c * 2 * CHUNK + kind * CHUNK, CHUNK), CHUNK), kind
         return pl.ds(pl.multiple_of(c * 2 * CHUNK, 2 * CHUNK), (kind - 1) * 2 * CHUNK), 0
 
-    def send(c, ahead, kind):
-        target = partner(ahead)
+    def send(c, target, kind):
         span, at = rows_of(c, kind)
         return pltpu.make_async_remote_copy(
             src_ref=sent.at[target, span], dst_ref=held.at[me, span],
@@ -312,19 +311,33 @@
                 )
         held[me, where_to, :] = sent[me, where_to, :]
 
-        def send_when(when, first, kind):
-            @pl.when(when)
-            def _():
-                for ahead in order:
-                    send(first, ahead, kind).start()
-
         @pl.when((c == 0) & (h == 0))
         def _():
             pl.semaphore_wait(barrier, narrow - 1 + wide - 1)
 
-        for first, kind in PIECES:
+        def sends(group, targets):
+            for target in targets:
+                @pl.when(me != target)
+                def _():
+                    for first, kind in group:
+                        send(first, target, kind).start()
+
+        for piece in PIECES:
+            first, kind = piece
             after = first + (kind == 3)
-            send_when((c == first) & (h == 0) if kind == 0 else (c == after) & (h == 1), first, kind)
+            done = (c == first) & (h == 0) if kind == 0 else (c == after) & (h == 1)
+
+            @pl.when(done)
+            def _():
+                if first >= chunks - 2:
+                    sends([piece], range(0, narrow, 2))
+                else:
+                    for ahead in order:
+                        send(first, partner(ahead), kind).start()
+
+        @pl.when((c == chunks - 1) & (h == 1))
+        def _():
+            sends([piece for piece in PIECES if piece[0] >= chunks - 2], range(1, narrow, 2))
 
     def tables(c):
         lanes = iota((8, 128), 1)
@@ -555,8 +568,8 @@
             both = waves_at(g, lambda n, span: doubled(coarse[n, span, chunk_here]), fine_of)
             where_to = pl.ds(pl.multiple_of(g * GROUP, GROUP), GROUP)
             for n, (high, part) in enumerate(both):
-                ready[h, n, where_to, :128] = jnp.where(low, high, part)
-                ready[h, n, where_to, 128:] = high
+                ready[c % 2, h, n, where_to, :128] = jnp.where(low, high, part)
+                ready[c % 2, h, n, where_to, 128:] = high
             return carry
 
         lax.fori_loop(0, half_lon // GROUP, one_group, 0)
@@ -570,8 +583,8 @@
 
         def one_group(g, carry):
             where_to = pl.ds(pl.multiple_of(g * LAST, LAST), LAST)
-            new_cos = dot(ready[h, 0, where_to, :], even)
-            new_sin = dot(ready[h, 1, where_to, :], odd)
+            new_cos = dot(ready[c % 2, h, 0, where_to, :], even)
+            new_sin = dot(ready[c % 2, h, 1, where_to, :], odd)
             if not last:
                 part_cos[where_to, :] += new_cos
                 part_sin[where_to, :] += new_sin
@@ -600,13 +613,13 @@
 
     angles_ahead(chunks - 2, 0)
     angles_ahead(chunks - 2, 1)
+    angles_ahead(chunks - 1, 0)
+    angles_ahead(chunks - 1, 1)
     for piece in PIECES:
         if piece[0] == chunks - 2:
             arrive(*piece)
     half_chunk(chunks - 2, 0, False)
     half_chunk(chunks - 2, 1, False)
-    angles_ahead(chunks - 1, 0)
-    angles_ahead(chunks - 1, 1)
     arrive(chunks - 1, 0)
     half_chunk(chunks - 1, 0, False)
     arrive(chunks - 1, 1)
@@ -639,7 +652,7 @@
         exchange(ahead, False).start()
     for ahead in range(1, narrow):
         for first, kind in PIECES:
-            send(first, ahead, kind).wait_send()
+            send(first, partner(ahead), kind).wait_send()
     best = peaks[pl.ds(pl.multiple_of(me_wide * REG_DEV, REG_DEV), REG_DEV), :]
     for ahead in range(1, wide):
         exchange(ahead, True).wait_recv()
@@ -682,7 +695,7 @@
             pltpu.VMEM((2 * members * lat, narrow * 128), jnp.bfloat16),
             pltpu.VMEM((narrow, chunks * 2 * CHUNK, lanes), jnp.float32),
             pltpu.VMEM((narrow, chunks * 2 * CHUNK, lanes), jnp.float32),
-            pltpu.VMEM((2, 2, lon // 2, 256), jnp.bfloat16),
+            pltpu.VMEM((2, 2, 2, lon // 2, 256), jnp.bfloat16),
             pltpu.VMEM((4, chunks * 128, 128), jnp.float32),
             pltpu.VMEM((2, FINE, chunks * 128), jnp.float32),
             pltpu.VMEM((2, FINE, chunks * 128), jnp.float32),

time: 75.6 us -> 74.7 us (0.988)
  Pallas kernels: 73.3 us -> 72.5 us
    pallas_call x1, Pallas kernels: 73.3 us -> 72.5 us  [per_device(): pl.pallas_call(functools.partial(fields_kernel, dims), in_specs=[hbm] * 5...]
where the time goes in v3:
time: 74.7 us; the launch traced here: 74.4 us
  Pallas kernels  72.5 us (97%)
  local copies, waits for them, and re-layouts  1.35 us (2%)
    pallas_call x1, Pallas kernels, per_device(): pl.pallas_call(functools.partial(fields_kernel, dims), in_specs=[hbm] * 5...  72.5 us

profile of v3, /device:TPU:8, one launch (start us, length us, event | category | flops | bytes accessed | tf_op | source)
XLA Modules:
  0.0 74.4 jit_solution(17858651245652674632)
XLA Ops:
  0.6 72.5 %shard_map.68 = f32[4,16,32]{2,1,0:T(8,128)} custom-call(s32[640]{0:T(1024)} %pair_hbm.1, s32[1,128]{1,0:T(1,128)} %bitcast.7, s32[16,128]{1,0:T(8,128)} %bitcast.6, bf16[2,4,160,2,1281]{4,3,2,1,0:T(2,128)(2,1)} %x_hbm.1, bf16[1281,80,128]{2,1,0:T(8,128)(2,1)} %bitcast.4), custom_call_target="tpu_custom_call" | custom-call | tf_op jit(solution)/shard_map/pallas_call | solution.py:680
  73.1 1.3 %fusion = (f32[2,32,16]{1,2,0:T(8,128)}, f32[2,32,16]{1,2,0:T(8,128)}) fusion(f32[4,32,16]{1,2,0:T(8,128)} %bitcast.5), kind=kLoop, calls=%fused_computation | loop fusion | bytes 16384 | tf_op jit(solution)/shard_map/slice | solution.py:727

commit v4 on v3

--- a/solution.py
+++ b/solution.py
@@ -101,9 +101,9 @@
 CHUNK = 16
 HALF = 8
 FINE = 32
-GROUP = 512
+GROUP = 1024
 FETCHES = 4
-LAST = 512
+LAST = 1024
 WIDEN = 32
 MESH = pl.DeviceIdType.MESH
 

time: 74.7 us -> 72.9 us (0.976)
  Pallas kernels: 72.5 us -> 70.7 us
    pallas_call x1, Pallas kernels: 72.5 us -> 70.7 us  [per_device(): pl.pallas_call(functools.partial(fields_kernel, dims), in_specs=[hbm] * 5...]
where the time goes in v4:
time: 72.9 us; the launch traced here: 72.7 us
  Pallas kernels  70.7 us (97%)
  local copies, waits for them, and re-layouts  1.35 us (2%)
    pallas_call x1, Pallas kernels, per_device(): pl.pallas_call(functools.partial(fields_kernel, dims), in_specs=[hbm] * 5...  70.7 us

profile of v4, /device:TPU:8, one launch (start us, length us, event | category | flops | bytes accessed | tf_op | source)
XLA Modules:
  0.0 72.7 jit_solution(7464724205373118214)
XLA Ops:
  0.6 70.7 %shard_map.68 = f32[4,16,32]{2,1,0:T(8,128)} custom-call(s32[640]{0:T(1024)} %pair_hbm.1, s32[1,128]{1,0:T(1,128)} %bitcast.7, s32[16,128]{1,0:T(8,128)} %bitcast.6, bf16[2,4,160,2,1281]{4,3,2,1,0:T(2,128)(2,1)} %x_hbm.1, bf16[1281,80,128]{2,1,0:T(8,128)(2,1)} %bitcast.4), custom_call_target="tpu_custom_call" | custom-call | tf_op jit(solution)/shard_map/pallas_call | solution.py:680
  71.3 1.3 %fusion = (f32[2,32,16]{1,2,0:T(8,128)}, f32[2,32,16]{1,2,0:T(8,128)}) fusion(f32[4,32,16]{1,2,0:T(8,128)} %bitcast.5), kind=kLoop, calls=%fused_computation | loop fusion | bytes 16384 | tf_op jit(solution)/shard_map/slice | solution.py:727

commit v5 on v4

--- a/solution.py
+++ b/solution.py
@@ -141,7 +141,7 @@
 def pieces_of(chunks):
     pieces = [(0, 0), (0, 1), (1, 2)]
     pieces += [(c, 3) for c in range(2, chunks - 2, 2)]
-    return pieces + [(chunks - 2, 2), (chunks - 1, 0), (chunks - 1, 1)]
+    return pieces + [(chunks - 2, 2), (chunks - 1, 2)]
 
 
 def fields_kernel(
@@ -574,17 +574,19 @@
 
         lax.fori_loop(0, half_lon // GROUP, one_group, 0)
 
-    def half_chunk(c, h, last):
-        here = pl.ds((c * 2 + h) * 64, 64)
-        (even_hi, even_lo), (odd_hi, odd_lo) = turned([(d, span_of(c, h)) for d in range(narrow)], here)
-        even = jnp.concatenate([even_hi, even_hi, even_lo, jnp.zeros_like(even_lo)], axis=0)
-        odd = jnp.concatenate([odd_hi, odd_hi, odd_lo, jnp.zeros_like(odd_lo)], axis=0)
+    def half_chunks(c, some, last):
+        evens, odds = [], []
+        for h in some:
+            here = pl.ds((c * 2 + h) * 64, 64)
+            (even_hi, even_lo), (odd_hi, odd_lo) = turned([(d, span_of(c, h)) for d in range(narrow)], here)
+            evens.append(jnp.concatenate([even_hi, even_hi, even_lo, jnp.zeros_like(even_lo)], axis=0))
+            odds.append(jnp.concatenate([odd_hi, odd_hi, odd_lo, jnp.zeros_like(odd_lo)], axis=0))
         sign = jnp.where(iota((LAST, 128), 1) < 64, 1.0, -1.0)
 
         def one_group(g, carry):
             where_to = pl.ds(pl.multiple_of(g * LAST, LAST), LAST)
-            new_cos = dot(ready[c % 2, h, 0, where_to, :], even)
-            new_sin = dot(ready[c % 2, h, 1, where_to, :], odd)
+            new_cos = sum(dot(ready[c % 2, h, 0, where_to, :], even) for h, even in zip(some, evens))
+            new_sin = sum(dot(ready[c % 2, h, 1, where_to, :], odd) for h, odd in zip(some, odds))
             if not last:
                 part_cos[where_to, :] += new_cos
                 part_sin[where_to, :] += new_sin
@@ -618,12 +620,9 @@
     for piece in PIECES:
         if piece[0] == chunks - 2:
             arrive(*piece)
-    half_chunk(chunks - 2, 0, False)
-    half_chunk(chunks - 2, 1, False)
-    arrive(chunks - 1, 0)
-    half_chunk(chunks - 1, 0, False)
-    arrive(chunks - 1, 1)
-    half_chunk(chunks - 1, 1, True)
+    half_chunks(chunks - 2, (0, 1), False)
+    arrive(chunks - 1, 2)
+    half_chunks(chunks - 1, (0, 1), True)
 
     def chosen(picks, values, missing):
         high, low = split(values)

time: 72.9 us -> 72.7 us (level)
  no operation moved by 1% of the time
where the time goes in v5:
time: 72.7 us; the launch traced here: 72.4 us
  Pallas kernels  70.4 us (97%)
  local copies, waits for them, and re-layouts  1.35 us (2%)
    pallas_call x1, Pallas kernels, per_device(): pl.pallas_call(functools.partial(fields_kernel, dims), in_specs=[hbm] * 5...  70.4 us

profile of v5, /device:TPU:8, one launch (start us, length us, event | category | flops | bytes accessed | tf_op | source)
XLA Modules:
  0.0 72.4 jit_solution(2364586332971110075)
XLA Ops:
  0.6 70.4 %shard_map.68 = f32[4,16,32]{2,1,0:T(8,128)} custom-call(s32[640]{0:T(1024)} %pair_hbm.1, s32[1,128]{1,0:T(1,128)} %bitcast.7, s32[16,128]{1,0:T(8,128)} %bitcast.6, bf16[2,4,160,2,1281]{4,3,2,1,0:T(2,128)(2,1)} %x_hbm.1, bf16[1281,80,128]{2,1,0:T(8,128)(2,1)} %bitcast.4), custom_call_target="tpu_custom_call" | custom-call | tf_op jit(solution)/shard_map/pallas_call | solution.py:679
  71.0 1.3 %fusion = (f32[2,32,16]{1,2,0:T(8,128)}, f32[2,32,16]{1,2,0:T(8,128)}) fusion(f32[4,32,16]{1,2,0:T(8,128)} %bitcast.5), kind=kLoop, calls=%fused_computation | loop fusion | bytes 16384 | tf_op jit(solution)/shard_map/slice | solution.py:726
